TPU v7x, 256 devices: a whole 4x4x8 slice. The times are simulated.
256 devices in a mesh: row: 16 (over z, core), col: 16 (over x, y).
Axes of the slice: x: 4, y: 4, z: 8, core: 2. Of those that a mesh axis runs over, the one named last changes fastest.
Arguments:
- cost_tiles: float32 [16, 16, 64, 128, 128], P('row', 'col'), may hold values from 0 to 66
- tile_rows: int32 [16, 16, 64], P('row', 'col'), may hold values from 0 to 127, as said below
- tile_cols: int32 [16, 16, 64], P('row', 'col'), may hold values from 0 to 127
- tile_count: int32 [16, 16], P('row', 'col'), may hold values from 16 to 64, as said below
- source_logmass: float32 [262144], P('row'), may hold values from -3 to 0
- target_logmass: float32 [262144], P('col'), may hold values from -103 to -100
- target_init: float32 [262144], P('col'), may hold values from -2 to 14
Outputs:
- source_potential: float32 [262144], P('row')
- target_potential: float32 [262144], P('col')
Inputs may be any that keep to these rules, and one draw needn't show every extreme that they name: Among the first tile_count slots of a device all (tile_rows, tile_cols) pairs differ; every source block of a row shard appears in such a slot of some device of that shard, and every target block of a col shard likewise. Slots at tile_count or later hold pairs to be ignored. `tile_count`: some device has all 64 slots in use in every draw.
All inputs are finite; a program needn't handle non-finite values.
Results may differ from a plain program's by a relative error of at most 0.00019.
Values sent between devices are 32-bit elements; how exact they have to be, the bound alone decides.
No kernel may reach another device: no remote copies, remote signals or barrier semaphores. Data moves between devices by JAX's collectives and lax.ppermute only.
A program may use at most 64 MiB of HBM per device.

v0:
```python
import jax
import jax.numpy as jnp
from jax import lax
from jax.sharding import PartitionSpec as P

ITERS = 2
EPS = 0.1


def copy_for_each(shard, axis):
    peers = lax.axis_size(axis)
    return lax.all_to_all(
        jnp.broadcast_to(shard[None], (peers, *shard.shape)), axis, 0, 0, tiled=True
    )


def of_everyone(shard, axis):
    everything = copy_for_each(shard, axis)
    return jnp.max(everything, axis=0)


def cut_along(shard, dim, peers):
    before, after = (shard.shape[:dim], shard.shape[dim + 1 :])
    return jnp.moveaxis(shard.reshape(*before, peers, -1, *after), dim, 0)


def sent_and_summed(shard, axis, dim):
    peers = lax.axis_size(axis)
    parts = lax.all_to_all(cut_along(shard, dim, peers), axis, 0, 0, tiled=True)
    return jnp.sum(parts, axis=0)


def in_order(parts, dim):
    shape = list(parts.shape[1:])
    shape[dim] *= parts.shape[0]
    return jnp.moveaxis(parts, 0, dim).reshape(shape)


def gathered_copies(shard, axis, dim):
    parts = copy_for_each(shard, axis)
    return in_order(parts, dim)


def block_stats(cost, pot_blocks, gather_ids, seg_ids, valid, nseg, rows_side):
    red = 2 if rows_side else 1
    part = pot_blocks[gather_ids]
    if rows_side:
        scores = (part[:, None, :] - cost) / EPS
    else:
        scores = (part[:, :, None] - cost) / EPS
    tmax = jnp.where(valid[:, None], jnp.max(scores, axis=red), -jnp.inf)
    onehot = (seg_ids[:, None] == jnp.arange(nseg)[None, :]) & valid[:, None]
    peak = jnp.max(jnp.where(onehot.T[:, :, None], tmax[None, :, :], -jnp.inf), axis=1)
    shift = jnp.where(valid[:, None], peak[seg_ids], 0.0)
    if rows_side:
        expo = jnp.exp(scores - shift[:, :, None])
    else:
        expo = jnp.exp(scores - shift[:, None, :])
    tsum = jnp.where(valid[:, None], jnp.sum(expo, axis=red), 0.0)
    mass = jnp.dot(
        onehot.astype(jnp.float32).T,
        tsum,
        precision=lax.Precision.HIGHEST,
        preferred_element_type=jnp.float32,
    )
    return (peak, mass)


def local_stats(cost, pot, gather_ids, seg_ids, count, nseg, rows_side):
    pot_blocks = pot.reshape(-1, cost.shape[-1])
    slots = cost.shape[0]
    valid = jnp.arange(slots) < count
    return block_stats(cost, pot_blocks, gather_ids, seg_ids, valid, nseg, rows_side)


def finish_source(peak, mass, logmass):
    top = of_everyone(peak, "col")
    scaled = mass * jnp.exp(peak - top)
    share = sent_and_summed(scaled.reshape(-1), "col", 0)
    width = share.shape[0]
    start = lax.axis_index("col") * width
    top_share = lax.dynamic_slice_in_dim(top.reshape(-1), start, width, 0)
    mass_share = lax.dynamic_slice_in_dim(logmass, start, width, 0)
    piece = EPS * mass_share - EPS * (top_share + jnp.log(share))
    return gathered_copies(piece, "col", 0)


def finish_target(peak, mass, logmass):
    top = of_everyone(peak, "row")
    scaled = mass * jnp.exp(peak - top)
    share = sent_and_summed(scaled.reshape(-1), "row", 0)
    width = share.shape[0]
    start = lax.axis_index("row") * width
    top_share = lax.dynamic_slice_in_dim(top.reshape(-1), start, width, 0)
    mass_share = lax.dynamic_slice_in_dim(logmass, start, width, 0)
    piece = EPS * mass_share - EPS * (top_share + jnp.log(share))
    return lax.all_gather(piece, "row", axis=0, tiled=True)


def local(
    cost_tiles, tile_rows, tile_cols, tile_count, source_logmass, target_logmass, target_init
):
    width = cost_tiles.shape[-1]
    cost = cost_tiles.reshape(cost_tiles.shape[2], width, width)
    rows = tile_rows.reshape(-1)
    cols = tile_cols.reshape(-1)
    count = tile_count.reshape(())
    src_blocks = source_logmass.shape[0] // width
    tgt_blocks = target_logmass.shape[0] // width
    target_potential = target_init
    source_potential = source_logmass
    for step in range(ITERS):
        peak, mass = local_stats(cost, target_potential, cols, rows, count, src_blocks, True)
        source_potential = finish_source(peak, mass, source_logmass)
        peak, mass = local_stats(cost, source_potential, rows, cols, count, tgt_blocks, False)
        target_potential = finish_target(peak, mass, target_logmass)
    return (source_potential, target_potential)


def solution(mesh):
    return jax.shard_map(
        local,
        mesh=mesh,
        in_specs=(
            P("row", "col", None, None, None),
            P("row", "col", None),
            P("row", "col", None),
            P("row", "col"),
            P("row"),
            P("col"),
            P("col"),
        ),
        out_specs=(P("row"), P("col")),
        check_vma=False,
    )
```

profile of v0, /device:TPU:1, one launch (start us, length us, event | category | flops | bytes accessed | tf_op | source)
XLA Modules:
  0.0 249.2 jit_solution(4396380979940419612)
XLA Ops:
  1.4 0.7 fusion.32
  2.0 0.6 gather_fusion
  2.6 3.3 %fusion.7 = f32[64,128]{1,0:T(8,128)S(1)} fusion(f32[1,1,64,128,128]{4,3,2,1,0:T(8,128)} %param.7, f32[64,128]{1,0:T(8,128)S(1)} %gather_fusion), kind=kLoop, calls=%fused_computation.27 | loop fusion | flops 3137536 | bytes 4259840 | tf_op jit(solution)/shard_map/reduce_max | solution.py:51
  6.0 0.1 broadcast_select_fusion.7
  6.1 1.6 select_reduce_fusion.3
  7.7 1.1 broadcast_in_dim.190
  8.8 7.6 %all-to-all-start = ((f32[16,128,128]{2,1,0:T(8,128)}), f32[16,128,128]{2,1,0:T(8,128)S(1)}, u32[]{:S(2)}, u32[]{:S(2)}) async-start(f32[16,128,128]{2,1,0:T(8,128)} %broadcast_in_dim.190), calls=%async_computation | async-start | bytes 2097152 | tf_op jit(solution)/shard_map/all_to_all | solution.py:12
  16.4 0.6 gather_fusion.1
  17.0 0.1 broadcast_select_fusion.3
  17.1 4.0 %exponential_reduce_fusion.3 = f32[64,128]{1,0:T(8,128)S(1)} fusion(f32[1,1,64,128,128]{4,3,2,1,0:T(8,128)} %param.7, f32[64,128]{1,0:T(8,128)S(1)} %broadcast_select_fusion.3, f32[64,128]{1,0:T(8,128)S(1)} %gather_fusion), kind=kLoop, calls=%fused_computation.22 | loop fusion | flops 4186112 | bytes 4292608 | tf_op jit(solution)/shard_map/reduce_sum | solution.py:59
  21.1 11.0 %all-to-all-done = f32[16,128,128]{2,1,0:T(8,128)S(1)} async-done(((f32[16,128,128]{2,1,0:T(8,128)}), f32[16,128,128]{2,1,0:T(8,128)S(1)}, u32[]{:S(2)}, u32[]{:S(2)}) %all-to-all-start) | async-done | bytes 1048608 | tf_op jit(solution)/shard_map/all_to_all | solution.py:12
  32.1 0.1 reduce_max.110
  32.1 1.0 convolution_multiply_fusion.3
  33.1 3.9 %all-to-all-start.1 = ((f32[16,1,1024]{2,1,0:T(1,128)}), f32[16,1,1024]{2,1,0:T(1,128)S(1)}, u32[]{:S(2)}, u32[]{:S(2)}) async-start(f32[16,1,1024]{2,1,0:T(1,128)} %bitcast.10), calls=%async_computation.1 | async-start | bytes 131072 | tf_op jit(solution)/shard_map/all_to_all | solution.py:29
  37.0 6.5 %all-to-all-done.1 = f32[16,1,1024]{2,1,0:T(1,128)S(1)} async-done(((f32[16,1,1024]{2,1,0:T(1,128)}), f32[16,1,1024]{2,1,0:T(1,128)S(1)}, u32[]{:S(2)}, u32[]{:S(2)}) %all-to-all-start.1) | async-done | bytes 65568 | tf_op jit(solution)/shard_map/all_to_all | solution.py:29
  43.6 0.7 multiply_subtract_fusion.3
  44.3 9.5 %all_to_all.68 = f32[16,1,1024]{2,1,0:T(1,128)S(1)} all-to-all(f32[16,1,1024]{2,1,0:T(1,128)S(1)} %broadcast_in_dim.192), channel_id=1, replica_groups=mesh['row'=16,'col'=16] {'col'}, dimensions={0} | all-to-all | bytes 131072 | tf_op jit(solution)/shard_map/all_to_all | solution.py:12
  53.8 0.6 gather_fusion.2
  54.4 2.9 %fusion.6 = f32[64,128]{1,0:T(8,128)S(1)} fusion(f32[1,1,64,128,128]{4,3,2,1,0:T(8,128)} %param.7, f32[64,128]{1,0:T(8,128)S(1)} %gather_fusion.2), kind=kLoop, calls=%fused_computation.26 | loop fusion | flops 3137536 | bytes 4259840 | tf_op jit(solution)/shard_map/reduce_max | solution.py:51
  57.2 0.1 broadcast_select_fusion.6
  57.3 1.6 select_reduce_fusion.2
  58.9 1.1 broadcast_in_dim.194
  60.0 13.7 %all-to-all-start.3 = ((f32[16,128,128]{2,1,0:T(8,128)}), f32[16,128,128]{2,1,0:T(8,128)S(1)}, u32[]{:S(2)}, u32[]{:S(2)}) async-start(f32[16,128,128]{2,1,0:T(8,128)} %broadcast_in_dim.194), calls=%async_computation.3 | async-start | bytes 2097152 | tf_op jit(solution)/shard_map/all_to_all | solution.py:12
  73.7 0.6 gather_fusion.3
  74.3 0.1 broadcast_select_fusion.2
  74.3 2.9 %exponential_reduce_fusion.2 = f32[64,128]{1,0:T(8,128)S(1)} fusion(f32[1,1,64,128,128]{4,3,2,1,0:T(8,128)} %param.7, f32[64,128]{1,0:T(8,128)S(1)} %broadcast_select_fusion.2, f32[64,128]{1,0:T(8,128)S(1)} %gather_fusion.2), kind=kLoop, calls=%fused_computation.20 | loop fusion | flops 4186112 | bytes 4292608 | tf_op jit(solution)/shard_map/reduce_sum | solution.py:59
  77.3 24.4 %all-to-all-done.3 = f32[16,128,128]{2,1,0:T(8,128)S(1)} async-done(((f32[16,128,128]{2,1,0:T(8,128)}), f32[16,128,128]{2,1,0:T(8,128)S(1)}, u32[]{:S(2)}, u32[]{:S(2)}) %all-to-all-start.3) | async-done | bytes 1048608 | tf_op jit(solution)/shard_map/all_to_all | solution.py:12
  101.7 1.0 convolution_multiply_fusion.2
  102.7 3.4 %all-to-all-start.4 = ((f32[16,1,1024]{2,1,0:T(1,128)}), f32[16,1,1024]{2,1,0:T(1,128)S(1)}, u32[]{:S(2)}, u32[]{:S(2)}) async-start(f32[16,1,1024]{2,1,0:T(1,128)} %bitcast.13), calls=%async_computation.4 | async-start | bytes 131072 | tf_op jit(solution)/shard_map/all_to_all | solution.py:29
  106.1 7.8 %all-to-all-done.4 = f32[16,1,1024]{2,1,0:T(1,128)S(1)} async-done(((f32[16,1,1024]{2,1,0:T(1,128)}), f32[16,1,1024]{2,1,0:T(1,128)S(1)}, u32[]{:S(2)}, u32[]{:S(2)}) %all-to-all-start.4) | async-done | bytes 65568 | tf_op jit(solution)/shard_map/all_to_all | solution.py:29
  113.9 0.7 multiply_subtract_fusion.2
  114.6 14.9 %all_gather.6 = f32[16384]{0:T(1024)S(1)} all-gather(f32[1024]{0:T(1024)S(1)} %multiply_subtract_fusion.2), channel_id=1, replica_groups=mesh['row'=16,'col'=16] {'row'}, dimensions={0}, use_global_device_ids=true | all-gather | bytes 69632 | tf_op jit(solution)/shard_map/all_gather | solution.py:97
  129.5 0.6 gather_fusion.4
  130.1 3.3 %fusion.5 = f32[64,128]{1,0:T(8,128)S(1)} fusion(f32[1,1,64,128,128]{4,3,2,1,0:T(8,128)} %param.7, f32[64,128]{1,0:T(8,128)S(1)} %gather_fusion.4), kind=kLoop, calls=%fused_computation.25 | loop fusion | flops 3137536 | bytes 4259840 | tf_op jit(solution)/shard_map/reduce_max | solution.py:51
  133.4 0.1 broadcast_select_fusion.5
  133.5 1.6 select_reduce_fusion.1
  135.1 1.1 broadcast_in_dim.196
  136.2 3.7 %all-to-all-start.5 = ((f32[16,128,128]{2,1,0:T(8,128)}), f32[16,128,128]{2,1,0:T(8,128)S(1)}, u32[]{:S(2)}, u32[]{:S(2)}) async-start(f32[16,128,128]{2,1,0:T(8,128)} %broadcast_in_dim.196), calls=%async_computation.5 | async-start | bytes 2097152 | tf_op jit(solution)/shard_map/all_to_all | solution.py:12
  139.9 0.6 gather_fusion.5
  140.5 0.1 broadcast_select_fusion.1
  140.6 4.0 %exponential_reduce_fusion.1 = f32[64,128]{1,0:T(8,128)S(1)} fusion(f32[1,1,64,128,128]{4,3,2,1,0:T(8,128)} %param.7, f32[64,128]{1,0:T(8,128)S(1)} %broadcast_select_fusion.1, f32[64,128]{1,0:T(8,128)S(1)} %gather_fusion.4), kind=kLoop, calls=%fused_computation.18 | loop fusion | flops 4186112 | bytes 4292608 | tf_op jit(solution)/shard_map/reduce_sum | solution.py:59
  144.5 12.5 %all-to-all-done.5 = f32[16,128,128]{2,1,0:T(8,128)S(1)} async-done(((f32[16,128,128]{2,1,0:T(8,128)}), f32[16,128,128]{2,1,0:T(8,128)S(1)}, u32[]{:S(2)}, u32[]{:S(2)}) %all-to-all-start.5) | async-done | bytes 1048608 | tf_op jit(solution)/shard_map/all_to_all | solution.py:12
  157.1 0.3 convolution_multiply_fusion.1
  157.4 9.8 %all_to_all.69 = f32[16,1,1024]{2,1,0:T(1,128)S(1)} all-to-all(f32[16,1,1024]{2,1,0:T(1,128)S(1)} %bitcast.63), channel_id=1, replica_groups=mesh['row'=16,'col'=16] {'col'}, dimensions={0} | all-to-all | bytes 131072 | tf_op jit(solution)/shard_map/all_to_all | solution.py:29
  167.3 0.7 multiply_subtract_fusion.1
  168.0 9.8 %all_to_all.70 = f32[16,1,1024]{2,1,0:T(1,128)S(1)} all-to-all(f32[16,1,1024]{2,1,0:T(1,128)S(1)} %broadcast_in_dim.197), channel_id=1, replica_groups=mesh['row'=16,'col'=16] {'col'}, dimensions={0} | all-to-all | bytes 131072 | tf_op jit(solution)/shard_map/all_to_all | solution.py:12
  177.8 0.6 gather_fusion.6
  178.4 2.8 %fusion.4 = f32[64,128]{1,0:T(8,128)S(1)} fusion(f32[1,1,64,128,128]{4,3,2,1,0:T(8,128)} %param.7, f32[64,128]{1,0:T(8,128)S(1)} %gather_fusion.6), kind=kLoop, calls=%fused_computation.24 | loop fusion | flops 3137536 | bytes 4259840 | tf_op jit(solution)/shard_map/reduce_max | solution.py:51
  181.2 0.1 broadcast_select_fusion.4
  181.3 1.6 select_reduce_fusion
  182.9 1.1 broadcast_in_dim.199
  184.0 8.1 %all-to-all-start.8 = ((f32[16,128,128]{2,1,0:T(8,128)}), f32[16,128,128]{2,1,0:T(8,128)S(1)}, u32[]{:S(2)}, u32[]{:S(2)}) async-start(f32[16,128,128]{2,1,0:T(8,128)} %broadcast_in_dim.199), calls=%async_computation.8 | async-start | bytes 2097152 | tf_op jit(solution)/shard_map/all_to_all | solution.py:12
  192.1 0.6 gather_fusion.7
  192.7 0.1 broadcast_select_fusion
  192.8 2.9 %exponential_reduce_fusion = f32[64,128]{1,0:T(8,128)S(1)} fusion(f32[1,1,64,128,128]{4,3,2,1,0:T(8,128)} %param.7, f32[64,128]{1,0:T(8,128)S(1)} %broadcast_select_fusion, f32[64,128]{1,0:T(8,128)S(1)} %gather_fusion.6), kind=kLoop, calls=%fused_computation.16 | loop fusion | flops 4186112 | bytes 4292608 | tf_op jit(solution)/shard_map/reduce_sum | solution.py:59
  195.7 24.4 %all-to-all-done.8 = f32[16,128,128]{2,1,0:T(8,128)S(1)} async-done(((f32[16,128,128]{2,1,0:T(8,128)}), f32[16,128,128]{2,1,0:T(8,128)S(1)}, u32[]{:S(2)}, u32[]{:S(2)}) %all-to-all-start.8) | async-done | bytes 1048608 | tf_op jit(solution)/shard_map/all_to_all | solution.py:12
  220.1 0.1 reduce_max.119
  220.1 1.0 convolution_multiply_fusion
  221.1 3.4 %all-to-all-start.9 = ((f32[16,1,1024]{2,1,0:T(1,128)}), f32[16,1,1024]{2,1,0:T(1,128)S(1)}, u32[]{:S(2)}, u32[]{:S(2)}) async-start(f32[16,1,1024]{2,1,0:T(1,128)} %bitcast.20), calls=%async_computation.9 | async-start | bytes 131072 | tf_op jit(solution)/shard_map/all_to_all | solution.py:29
  224.5 7.8 %all-to-all-done.9 = f32[16,1,1024]{2,1,0:T(1,128)S(1)} async-done(((f32[16,1,1024]{2,1,0:T(1,128)}), f32[16,1,1024]{2,1,0:T(1,128)S(1)}, u32[]{:S(2)}, u32[]{:S(2)}) %all-to-all-start.9) | async-done | bytes 65568 | tf_op jit(solution)/shard_map/all_to_all | solution.py:29
  232.4 0.7 multiply_subtract_fusion
  233.1 14.9 %all_gather.7 = f32[16384]{0:T(1024)S(1)} all-gather(f32[1024]{0:T(1024)S(1)} %multiply_subtract_fusion), channel_id=1, replica_groups=mesh['row'=16,'col'=16] {'row'}, dimensions={0}, use_global_device_ids=true | all-gather | bytes 69632 | tf_op jit(solution)/shard_map/all_gather | solution.py:97
  247.9 0.6 copy.20
  248.6 0.6 copy.21
  (19 shorter events, 0.5 us)
Async XLA Ops:
  0.6 1.4 copy-start
  0.6 5.4 %copy-start.2 = (s32[1,1,64]{2,1,0:T(1,128)S(1)}, s32[1,1,64]{2,1,0:T(1,128)}, u32[]{:S(2)}) copy-start(s32[1,1,64]{2,1,0:T(1,128)} %param.9) | copy-start | bytes 772
  0.7 5.4 %copy-start.1 = (s32[1,1,64]{2,1,0:T(1,128)S(1)}, s32[1,1,64]{2,1,0:T(1,128)}, u32[]{:S(2)}) copy-start(s32[1,1,64]{2,1,0:T(1,128)} %param.8) | copy-start | bytes 772
  8.8 23.2 %all-to-all-start = ((f32[16,128,128]{2,1,0:T(8,128)}), f32[16,128,128]{2,1,0:T(8,128)S(1)}, u32[]{:S(2)}, u32[]{:S(2)}) async-start(f32[16,128,128]{2,1,0:T(8,128)} %broadcast_in_dim.190), calls=%async_computation | async-start | bytes 2097152 | tf_op jit(solution)/shard_map/all_to_all | solution.py:12
  33.1 10.4 %all-to-all-start.1 = ((f32[16,1,1024]{2,1,0:T(1,128)}), f32[16,1,1024]{2,1,0:T(1,128)S(1)}, u32[]{:S(2)}, u32[]{:S(2)}) async-start(f32[16,1,1024]{2,1,0:T(1,128)} %bitcast.10), calls=%async_computation.1 | async-start | bytes 131072 | tf_op jit(solution)/shard_map/all_to_all | solution.py:29
  60.0 41.7 %all-to-all-start.3 = ((f32[16,128,128]{2,1,0:T(8,128)}), f32[16,128,128]{2,1,0:T(8,128)S(1)}, u32[]{:S(2)}, u32[]{:S(2)}) async-start(f32[16,128,128]{2,1,0:T(8,128)} %broadcast_in_dim.194), calls=%async_computation.3 | async-start | bytes 2097152 | tf_op jit(solution)/shard_map/all_to_all | solution.py:12
  102.7 11.2 %all-to-all-start.4 = ((f32[16,1,1024]{2,1,0:T(1,128)}), f32[16,1,1024]{2,1,0:T(1,128)S(1)}, u32[]{:S(2)}, u32[]{:S(2)}) async-start(f32[16,1,1024]{2,1,0:T(1,128)} %bitcast.13), calls=%async_computation.4 | async-start | bytes 131072 | tf_op jit(solution)/shard_map/all_to_all | solution.py:29
  136.2 20.8 %all-to-all-start.5 = ((f32[16,128,128]{2,1,0:T(8,128)}), f32[16,128,128]{2,1,0:T(8,128)S(1)}, u32[]{:S(2)}, u32[]{:S(2)}) async-start(f32[16,128,128]{2,1,0:T(8,128)} %broadcast_in_dim.196), calls=%async_computation.5 | async-start | bytes 2097152 | tf_op jit(solution)/shard_map/all_to_all | solution.py:12
  184.0 36.1 %all-to-all-start.8 = ((f32[16,128,128]{2,1,0:T(8,128)}), f32[16,128,128]{2,1,0:T(8,128)S(1)}, u32[]{:S(2)}, u32[]{:S(2)}) async-start(f32[16,128,128]{2,1,0:T(8,128)} %broadcast_in_dim.199), calls=%async_computation.8 | async-start | bytes 2097152 | tf_op jit(solution)/shard_map/all_to_all | solution.py:12
  221.1 11.2 %all-to-all-start.9 = ((f32[16,1,1024]{2,1,0:T(1,128)}), f32[16,1,1024]{2,1,0:T(1,128)S(1)}, u32[]{:S(2)}, u32[]{:S(2)}) async-start(f32[16,1,1024]{2,1,0:T(1,128)} %bitcast.20), calls=%async_computation.9 | async-start | bytes 131072 | tf_op jit(solution)/shard_map/all_to_all | solution.py:29
where the time goes:
time: 250 us; the launch traced here: 249 us
  waiting for transfers between devices  94.4 us (38%)
  blocking collectives  58.7 us (23%)
  starting transfers between devices  43.8 us (18%)
  other arithmetic  37.1 us (15%)
  local copies, waits for them, and re-layouts  10.5 us (4%)
  matrix products  3.19 us (1%)
    all_to_all x4, waiting for transfers between devices, copy_for_each(): lax.all_to_all(jnp.broadcast_to(shard[None], (peers, *shard.shape)), axis...  72.3 us
    all_to_all x4, starting transfers between devices, copy_for_each(): lax.all_to_all(jnp.broadcast_to(shard[None], (peers, *shard.shape)), axis...  33 us
    all_gather x2, blocking collectives, finish_target(): return lax.all_gather(piece, 'row', axis=0, tiled=True)  29.7 us
    all_to_all x3, waiting for transfers between devices, sent_and_summed(): parts = lax.all_to_all(cut_along(shard, dim, peers), axis, 0, 0, tiled=True)  22.1 us
    all_to_all x2, blocking collectives, copy_for_each(): lax.all_to_all(jnp.broadcast_to(shard[None], (peers, *shard.shape)), axis...  19.2 us
    reduce_sum x4, other arithmetic, block_stats(): tsum = jnp.where(valid[:, None], jnp.sum(expo, axis=red), 0.0)  13.8 us
    reduce_max x4, other arithmetic, block_stats(): tmax = jnp.where(valid[:, None], jnp.max(scores, axis=red), -jnp.inf)  12.4 us
    all_to_all x3, starting transfers between devices, sent_and_summed(): parts = lax.all_to_all(cut_along(shard, dim, peers), axis, 0, 0, tiled=True)  10.8 us
  transfers between devices with their start and end apart: 7, of which 7 were waited for; matrix products, arithmetic and copies ran while one was open for 7% of the time, Pallas kernels for 0%

commit v1 on v0

--- a/solution.py
+++ b/solution.py
@@ -94,7 +94,9 @@
     top_share = lax.dynamic_slice_in_dim(top.reshape(-1), start, width, 0)
     mass_share = lax.dynamic_slice_in_dim(logmass, start, width, 0)
     piece = EPS * mass_share - EPS * (top_share + jnp.log(share))
-    return lax.all_gather(piece, "row", axis=0, tiled=True)
+    return jnp.concatenate(
+        lax.all_to_all(jnp.stack([piece] * lax.axis_size("row")), "row", 0, 0), axis=0
+    )
 
 
 def local(

time: 250 us -> 241 us (0.964)
  blocking collectives: 58.7 us -> 50.3 us
    all_gather x2 -> x0, blocking collectives: 29.7 us -> none  [finish_target(): return lax.all_gather(piece, 'row', axis=0, tiled=True)]
    all_to_all x1 -> x2, blocking collectives: 9.76 us -> 20.7 us  [sent_and_summed(): parts = lax.all_to_all(cut_along(shard, dim, peers), axis, 0, 0, tiled=True)]
    all_to_all x0 -> x1, blocking collectives: none -> 10.3 us  [finish_target(): lax.all_to_all(jnp.stack([piece] * lax.axis_size('row')), 'row', 0, 0)]
    all_to_all x0 -> x1, waiting for transfers between devices: none -> 7.82 us  [finish_target(): lax.all_to_all(jnp.stack([piece] * lax.axis_size('row')), 'row', 0, 0)]
    all_to_all x3 -> x2, waiting for transfers between devices: 22.1 us -> 14.3 us  [sent_and_summed(): parts = lax.all_to_all(cut_along(shard, dim, peers), axis, 0, 0, tiled=True)]
    all_to_all x3 -> x2, starting transfers between devices: 10.8 us -> 7.33 us  [sent_and_summed(): parts = lax.all_to_all(cut_along(shard, dim, peers), axis, 0, 0, tiled=True)]
    all_to_all x0 -> x1, starting transfers between devices: none -> 3.41 us  [finish_target(): lax.all_to_all(jnp.stack([piece] * lax.axis_size('row')), 'row', 0, 0)]
where the time goes in v1:
time: 241 us; the launch traced here: 240 us
  waiting for transfers between devices  94.5 us (39%)
  blocking collectives  50.3 us (21%)
  starting transfers between devices  43 us (18%)
  other arithmetic  37.1 us (15%)
  local copies, waits for them, and re-layouts  11.2 us (5%)
  matrix products  2.56 us (1%)
    all_to_all x4, waiting for transfers between devices, copy_for_each(): lax.all_to_all(jnp.broadcast_to(shard[None], (peers, *shard.shape)), axis...  72.4 us
    all_to_all x4, starting transfers between devices, copy_for_each(): lax.all_to_all(jnp.broadcast_to(shard[None], (peers, *shard.shape)), axis...  32.2 us
    all_to_all x2, blocking collectives, sent_and_summed(): parts = lax.all_to_all(cut_along(shard, dim, peers), axis, 0, 0, tiled=True)  20.7 us
    all_to_all x2, blocking collectives, copy_for_each(): lax.all_to_all(jnp.broadcast_to(shard[None], (peers, *shard.shape)), axis...  19.2 us
    all_to_all x2, waiting for transfers between devices, sent_and_summed(): parts = lax.all_to_all(cut_along(shard, dim, peers), axis, 0, 0, tiled=True)  14.3 us
    reduce_sum x4, other arithmetic, block_stats(): tsum = jnp.where(valid[:, None], jnp.sum(expo, axis=red), 0.0)  13.8 us
    reduce_max x4, other arithmetic, block_stats(): tmax = jnp.where(valid[:, None], jnp.max(scores, axis=red), -jnp.inf)  12.4 us
    all_to_all x1, blocking collectives, finish_target(): lax.all_to_all(jnp.stack([piece] * lax.axis_size('row')), 'row', 0, 0)  10.3 us
  transfers between devices with their start and end apart: 7, of which 7 were waited for; matrix products, arithmetic and copies ran while one was open for 7% of the time, Pallas kernels for 0%

profile of v1, /device:TPU:1, one launch (start us, length us, event | category | flops | bytes accessed | tf_op | source)
XLA Modules:
  0.0 240.2 jit_solution(5336740138680823560)
XLA Ops:
  1.4 0.7 fusion.32
  2.0 0.6 gather_fusion
  2.6 3.3 %fusion.7 = f32[64,128]{1,0:T(8,128)S(1)} fusion(f32[1,1,64,128,128]{4,3,2,1,0:T(8,128)} %param.7, f32[64,128]{1,0:T(8,128)S(1)} %gather_fusion), kind=kLoop, calls=%fused_computation.27 | loop fusion | flops 3137536 | bytes 4259840 | tf_op jit(solution)/shard_map/reduce_max | solution.py:51
  6.0 0.1 broadcast_select_fusion.7
  6.1 1.6 select_reduce_fusion.3
  7.7 1.1 broadcast_in_dim.190
  8.8 7.6 %all-to-all-start = ((f32[16,128,128]{2,1,0:T(8,128)}), f32[16,128,128]{2,1,0:T(8,128)S(1)}, u32[]{:S(2)}, u32[]{:S(2)}) async-start(f32[16,128,128]{2,1,0:T(8,128)} %broadcast_in_dim.190), calls=%async_computation | async-start | bytes 2097152 | tf_op jit(solution)/shard_map/all_to_all | solution.py:12
  16.4 0.6 gather_fusion.1
  17.0 0.1 broadcast_select_fusion.3
  17.1 4.0 %exponential_reduce_fusion.3 = f32[64,128]{1,0:T(8,128)S(1)} fusion(f32[1,1,64,128,128]{4,3,2,1,0:T(8,128)} %param.7, f32[64,128]{1,0:T(8,128)S(1)} %broadcast_select_fusion.3, f32[64,128]{1,0:T(8,128)S(1)} %gather_fusion), kind=kLoop, calls=%fused_computation.22 | loop fusion | flops 4186112 | bytes 4292608 | tf_op jit(solution)/shard_map/reduce_sum | solution.py:59
  21.1 11.0 %all-to-all-done = f32[16,128,128]{2,1,0:T(8,128)S(1)} async-done(((f32[16,128,128]{2,1,0:T(8,128)}), f32[16,128,128]{2,1,0:T(8,128)S(1)}, u32[]{:S(2)}, u32[]{:S(2)}) %all-to-all-start) | async-done | bytes 1048608 | tf_op jit(solution)/shard_map/all_to_all | solution.py:12
  32.1 0.1 reduce_max.110
  32.1 1.0 convolution_multiply_fusion.3
  33.1 3.9 %all-to-all-start.1 = ((f32[16,1,1024]{2,1,0:T(1,128)}), f32[16,1,1024]{2,1,0:T(1,128)S(1)}, u32[]{:S(2)}, u32[]{:S(2)}) async-start(f32[16,1,1024]{2,1,0:T(1,128)} %bitcast.10), calls=%async_computation.1 | async-start | bytes 131072 | tf_op jit(solution)/shard_map/all_to_all | solution.py:29
  37.0 6.5 %all-to-all-done.1 = f32[16,1,1024]{2,1,0:T(1,128)S(1)} async-done(((f32[16,1,1024]{2,1,0:T(1,128)}), f32[16,1,1024]{2,1,0:T(1,128)S(1)}, u32[]{:S(2)}, u32[]{:S(2)}) %all-to-all-start.1) | async-done | bytes 65568 | tf_op jit(solution)/shard_map/all_to_all | solution.py:29
  43.6 0.7 multiply_subtract_fusion.3
  44.3 9.5 %all_to_all.80 = f32[16,1,1024]{2,1,0:T(1,128)S(1)} all-to-all(f32[16,1,1024]{2,1,0:T(1,128)S(1)} %broadcast_in_dim.192), channel_id=1, replica_groups=mesh['row'=16,'col'=16] {'col'}, dimensions={0} | all-to-all | bytes 131072 | tf_op jit(solution)/shard_map/all_to_all | solution.py:12
  53.8 0.6 gather_fusion.2
  54.4 2.9 %fusion.6 = f32[64,128]{1,0:T(8,128)S(1)} fusion(f32[1,1,64,128,128]{4,3,2,1,0:T(8,128)} %param.7, f32[64,128]{1,0:T(8,128)S(1)} %gather_fusion.2), kind=kLoop, calls=%fused_computation.26 | loop fusion | flops 3137536 | bytes 4259840 | tf_op jit(solution)/shard_map/reduce_max | solution.py:51
  57.2 0.1 broadcast_select_fusion.6
  57.3 1.6 select_reduce_fusion.2
  58.9 1.1 broadcast_in_dim.194
  60.0 13.7 %all-to-all-start.3 = ((f32[16,128,128]{2,1,0:T(8,128)}), f32[16,128,128]{2,1,0:T(8,128)S(1)}, u32[]{:S(2)}, u32[]{:S(2)}) async-start(f32[16,128,128]{2,1,0:T(8,128)} %broadcast_in_dim.194), calls=%async_computation.3 | async-start | bytes 2097152 | tf_op jit(solution)/shard_map/all_to_all | solution.py:12
  73.7 0.6 gather_fusion.3
  74.3 0.1 broadcast_select_fusion.2
  74.3 2.9 %exponential_reduce_fusion.2 = f32[64,128]{1,0:T(8,128)S(1)} fusion(f32[1,1,64,128,128]{4,3,2,1,0:T(8,128)} %param.7, f32[64,128]{1,0:T(8,128)S(1)} %broadcast_select_fusion.2, f32[64,128]{1,0:T(8,128)S(1)} %gather_fusion.2), kind=kLoop, calls=%fused_computation.20 | loop fusion | flops 4186112 | bytes 4292608 | tf_op jit(solution)/shard_map/reduce_sum | solution.py:59
  77.3 24.4 %all-to-all-done.3 = f32[16,128,128]{2,1,0:T(8,128)S(1)} async-done(((f32[16,128,128]{2,1,0:T(8,128)}), f32[16,128,128]{2,1,0:T(8,128)S(1)}, u32[]{:S(2)}, u32[]{:S(2)}) %all-to-all-start.3) | async-done | bytes 1048608 | tf_op jit(solution)/shard_map/all_to_all | solution.py:12
  101.7 1.0 convolution_multiply_fusion.2
  102.7 3.4 %all-to-all-start.4 = ((f32[16,1,1024]{2,1,0:T(1,128)}), f32[16,1,1024]{2,1,0:T(1,128)S(1)}, u32[]{:S(2)}, u32[]{:S(2)}) async-start(f32[16,1,1024]{2,1,0:T(1,128)} %bitcast.13), calls=%async_computation.4 | async-start | bytes 131072 | tf_op jit(solution)/shard_map/all_to_all | solution.py:29
  106.1 7.8 %all-to-all-done.4 = f32[16,1,1024]{2,1,0:T(1,128)S(1)} async-done(((f32[16,1,1024]{2,1,0:T(1,128)}), f32[16,1,1024]{2,1,0:T(1,128)S(1)}, u32[]{:S(2)}, u32[]{:S(2)}) %all-to-all-start.4) | async-done | bytes 65568 | tf_op jit(solution)/shard_map/all_to_all | solution.py:29
  113.9 0.7 multiply_subtract_fusion.2
  114.7 10.3 %all_to_all.81 = f32[16,1,1024]{2,1,0:T(1,128)S(1)} all-to-all(f32[16,1,1024]{2,1,0:T(1,128)S(1)} %stack.4), channel_id=1, replica_groups=mesh['row'=16,'col'=16] {'row'}, dimensions={0} | all-to-all | bytes 131072 | tf_op jit(solution)/shard_map/all_to_all | solution.py:98
  125.0 0.6 gather_fusion.4
  125.6 3.3 %fusion.5 = f32[64,128]{1,0:T(8,128)S(1)} fusion(f32[1,1,64,128,128]{4,3,2,1,0:T(8,128)} %param.7, f32[64,128]{1,0:T(8,128)S(1)} %gather_fusion.4), kind=kLoop, calls=%fused_computation.25 | loop fusion | flops 3137536 | bytes 4259840 | tf_op jit(solution)/shard_map/reduce_max | solution.py:51
  129.0 0.1 broadcast_select_fusion.5
  129.0 1.6 select_reduce_fusion.1
  130.7 1.1 broadcast_in_dim.196
  131.7 3.7 %all-to-all-start.6 = ((f32[16,128,128]{2,1,0:T(8,128)}), f32[16,128,128]{2,1,0:T(8,128)S(1)}, u32[]{:S(2)}, u32[]{:S(2)}) async-start(f32[16,128,128]{2,1,0:T(8,128)} %broadcast_in_dim.196), calls=%async_computation.6 | async-start | bytes 2097152 | tf_op jit(solution)/shard_map/all_to_all | solution.py:12
  135.4 0.6 gather_fusion.5
  136.0 0.1 broadcast_select_fusion.1
  136.1 4.0 %exponential_reduce_fusion.1 = f32[64,128]{1,0:T(8,128)S(1)} fusion(f32[1,1,64,128,128]{4,3,2,1,0:T(8,128)} %param.7, f32[64,128]{1,0:T(8,128)S(1)} %broadcast_select_fusion.1, f32[64,128]{1,0:T(8,128)S(1)} %gather_fusion.4), kind=kLoop, calls=%fused_computation.18 | loop fusion | flops 4186112 | bytes 4292608 | tf_op jit(solution)/shard_map/reduce_sum | solution.py:59
  140.1 12.5 %all-to-all-done.6 = f32[16,128,128]{2,1,0:T(8,128)S(1)} async-done(((f32[16,128,128]{2,1,0:T(8,128)}), f32[16,128,128]{2,1,0:T(8,128)S(1)}, u32[]{:S(2)}, u32[]{:S(2)}) %all-to-all-start.6) | async-done | bytes 1048608 | tf_op jit(solution)/shard_map/all_to_all | solution.py:12
  152.7 0.3 convolution_multiply_fusion.1
  153.0 9.7 %all_to_all.82 = f32[16,1,1024]{2,1,0:T(1,128)S(1)} all-to-all(f32[16,1,1024]{2,1,0:T(1,128)S(1)} %bitcast.65), channel_id=1, replica_groups=mesh['row'=16,'col'=16] {'col'}, dimensions={0} | all-to-all | bytes 131072 | tf_op jit(solution)/shard_map/all_to_all | solution.py:29
  162.8 0.7 multiply_subtract_fusion.1
  163.5 9.8 %all_to_all.83 = f32[16,1,1024]{2,1,0:T(1,128)S(1)} all-to-all(f32[16,1,1024]{2,1,0:T(1,128)S(1)} %broadcast_in_dim.197), channel_id=1, replica_groups=mesh['row'=16,'col'=16] {'col'}, dimensions={0} | all-to-all | bytes 131072 | tf_op jit(solution)/shard_map/all_to_all | solution.py:12
  173.3 0.6 gather_fusion.6
  173.9 2.8 %fusion.4 = f32[64,128]{1,0:T(8,128)S(1)} fusion(f32[1,1,64,128,128]{4,3,2,1,0:T(8,128)} %param.7, f32[64,128]{1,0:T(8,128)S(1)} %gather_fusion.6), kind=kLoop, calls=%fused_computation.24 | loop fusion | flops 3137536 | bytes 4259840 | tf_op jit(solution)/shard_map/reduce_max | solution.py:51
  176.8 0.1 broadcast_select_fusion.4
  176.8 1.6 select_reduce_fusion
  178.4 1.1 broadcast_in_dim.199
  179.5 7.3 %all-to-all-start.9 = ((f32[16,128,128]{2,1,0:T(8,128)}), f32[16,128,128]{2,1,0:T(8,128)S(1)}, u32[]{:S(2)}, u32[]{:S(2)}) async-start(f32[16,128,128]{2,1,0:T(8,128)} %broadcast_in_dim.199), calls=%async_computation.9 | async-start | bytes 2097152 | tf_op jit(solution)/shard_map/all_to_all | solution.py:12
  186.8 0.6 gather_fusion.7
  187.4 0.1 broadcast_select_fusion
  187.5 2.9 %exponential_reduce_fusion = f32[64,128]{1,0:T(8,128)S(1)} fusion(f32[1,1,64,128,128]{4,3,2,1,0:T(8,128)} %param.7, f32[64,128]{1,0:T(8,128)S(1)} %broadcast_select_fusion, f32[64,128]{1,0:T(8,128)S(1)} %gather_fusion.6), kind=kLoop, calls=%fused_computation.16 | loop fusion | flops 4186112 | bytes 4292608 | tf_op jit(solution)/shard_map/reduce_sum | solution.py:59
  190.4 24.5 %all-to-all-done.9 = f32[16,128,128]{2,1,0:T(8,128)S(1)} async-done(((f32[16,128,128]{2,1,0:T(8,128)}), f32[16,128,128]{2,1,0:T(8,128)S(1)}, u32[]{:S(2)}, u32[]{:S(2)}) %all-to-all-start.9) | async-done | bytes 1048608 | tf_op jit(solution)/shard_map/all_to_all | solution.py:12
  215.0 0.3 convolution_multiply_fusion
  215.3 11.0 %all_to_all.84 = f32[16,1,1024]{2,1,0:T(1,128)S(1)} all-to-all(f32[16,1,1024]{2,1,0:T(1,128)S(1)} %bitcast.64), channel_id=1, replica_groups=mesh['row'=16,'col'=16] {'row'}, dimensions={0} | all-to-all | bytes 131072 | tf_op jit(solution)/shard_map/all_to_all | solution.py:29
  226.3 0.7 multiply_subtract_fusion
  227.0 0.7 stack.5
  227.7 3.4 %all-to-all-start.11 = ((f32[16,1,1024]{2,1,0:T(1,128)}), f32[16,1,1024]{2,1,0:T(1,128)S(1)}, u32[]{:S(2)}, u32[]{:S(2)}) async-start(f32[16,1,1024]{2,1,0:T(1,128)} %stack.5), calls=%async_computation.11 | async-start | bytes 131072 | tf_op jit(solution)/shard_map/all_to_all | solution.py:98
  231.1 7.8 %all-to-all-done.11 = f32[16,1,1024]{2,1,0:T(1,128)S(1)} async-done(((f32[16,1,1024]{2,1,0:T(1,128)}), f32[16,1,1024]{2,1,0:T(1,128)S(1)}, u32[]{:S(2)}, u32[]{:S(2)}) %all-to-all-start.11) | async-done | bytes 65568 | tf_op jit(solution)/shard_map/all_to_all | solution.py:98
  238.9 0.6 copy.20
  239.6 0.6 copy.21
  (21 shorter events, 0.6 us)
Async XLA Ops:
  0.6 1.4 copy-start
  0.6 5.4 %copy-start.2 = (s32[1,1,64]{2,1,0:T(1,128)S(1)}, s32[1,1,64]{2,1,0:T(1,128)}, u32[]{:S(2)}) copy-start(s32[1,1,64]{2,1,0:T(1,128)} %param.9) | copy-start | bytes 772
  0.7 5.4 %copy-start.1 = (s32[1,1,64]{2,1,0:T(1,128)S(1)}, s32[1,1,64]{2,1,0:T(1,128)}, u32[]{:S(2)}) copy-start(s32[1,1,64]{2,1,0:T(1,128)} %param.8) | copy-start | bytes 772
  8.8 23.2 %all-to-all-start = ((f32[16,128,128]{2,1,0:T(8,128)}), f32[16,128,128]{2,1,0:T(8,128)S(1)}, u32[]{:S(2)}, u32[]{:S(2)}) async-start(f32[16,128,128]{2,1,0:T(8,128)} %broadcast_in_dim.190), calls=%async_computation | async-start | bytes 2097152 | tf_op jit(solution)/shard_map/all_to_all | solution.py:12
  33.1 10.4 %all-to-all-start.1 = ((f32[16,1,1024]{2,1,0:T(1,128)}), f32[16,1,1024]{2,1,0:T(1,128)S(1)}, u32[]{:S(2)}, u32[]{:S(2)}) async-start(f32[16,1,1024]{2,1,0:T(1,128)} %bitcast.10), calls=%async_computation.1 | async-start | bytes 131072 | tf_op jit(solution)/shard_map/all_to_all | solution.py:29
  60.0 41.7 %all-to-all-start.3 = ((f32[16,128,128]{2,1,0:T(8,128)}), f32[16,128,128]{2,1,0:T(8,128)S(1)}, u32[]{:S(2)}, u32[]{:S(2)}) async-start(f32[16,128,128]{2,1,0:T(8,128)} %broadcast_in_dim.194), calls=%async_computation.3 | async-start | bytes 2097152 | tf_op jit(solution)/shard_map/all_to_all | solution.py:12
  102.7 11.2 %all-to-all-start.4 = ((f32[16,1,1024]{2,1,0:T(1,128)}), f32[16,1,1024]{2,1,0:T(1,128)S(1)}, u32[]{:S(2)}, u32[]{:S(2)}) async-start(f32[16,1,1024]{2,1,0:T(1,128)} %bitcast.13), calls=%async_computation.4 | async-start | bytes 131072 | tf_op jit(solution)/shard_map/all_to_all | solution.py:29
  131.7 20.9 %all-to-all-start.6 = ((f32[16,128,128]{2,1,0:T(8,128)}), f32[16,128,128]{2,1,0:T(8,128)S(1)}, u32[]{:S(2)}, u32[]{:S(2)}) async-start(f32[16,128,128]{2,1,0:T(8,128)} %broadcast_in_dim.196), calls=%async_computation.6 | async-start | bytes 2097152 | tf_op jit(solution)/shard_map/all_to_all | solution.py:12
  179.5 35.4 %all-to-all-start.9 = ((f32[16,128,128]{2,1,0:T(8,128)}), f32[16,128,128]{2,1,0:T(8,128)S(1)}, u32[]{:S(2)}, u32[]{:S(2)}) async-start(f32[16,128,128]{2,1,0:T(8,128)} %broadcast_in_dim.199), calls=%async_computation.9 | async-start | bytes 2097152 | tf_op jit(solution)/shard_map/all_to_all | solution.py:12
  227.7 11.2 %all-to-all-start.11 = ((f32[16,1,1024]{2,1,0:T(1,128)}), f32[16,1,1024]{2,1,0:T(1,128)S(1)}, u32[]{:S(2)}, u32[]{:S(2)}) async-start(f32[16,1,1024]{2,1,0:T(1,128)} %stack.5), calls=%async_computation.11 | async-start | bytes 131072 | tf_op jit(solution)/shard_map/all_to_all | solution.py:98
